TPU v7x, 128 devices: a whole 4x4x4 slice. The times are simulated.
128 devices in a mesh: src: 4 (over x_lo, core), tgt: 32 (over y, x_hi, z).
Axes of the slice: x: 4 (x_hi: 2, x_lo: 2; x = x_hi * 2 + x_lo), y: 4, z: 4, core: 2. Of those that a mesh axis runs over, the one named last changes fastest.
Arguments:
- source_feat: bfloat16 [16384, 256], P(('src', 'tgt')), may hold values from -40 to 40
- target_feat: bfloat16 [57600, 256], P('tgt', 'src'), may hold values from -4 to 4
- proj: bfloat16 [256, 256], replicated, may hold values from -0.375 to 0.375
Outputs:
- flow: float32 [2, 16384], P(None, ('src', 'tgt'))
- matched: bfloat16 [16384, 256], P(('src', 'tgt'))
All inputs are finite; a program needn't handle non-finite values.
Results may differ from a plain program's by a relative error of at most 0.0075.
Values may be sent and summed in bfloat16 or wider, within the bound.
A program may use at most 256 MiB of HBM per device.

v0:
```python
import jax
import jax.numpy as jnp
from jax import lax
from jax.sharding import PartitionSpec as P

W_GRID = 320


def grid_coords(pos):
    return (
        (pos % W_GRID).astype(jnp.float32) / W_GRID,
        (pos // W_GRID).astype(jnp.float32) / W_GRID,
    )


def partial_block(queries, keys, key_start):
    width = queries.shape[1]
    scores = jnp.einsum("qc,kc->qk", queries, keys, preferred_element_type=jnp.float32) * width ** (
        -0.5
    )
    top = jnp.max(scores, axis=1)
    weights = jnp.exp(scores - top[:, None])
    total = jnp.sum(weights, axis=1)
    pos = key_start + jnp.arange(keys.shape[0], dtype=jnp.int32)
    grid_x, grid_y = grid_coords(pos)
    coord_sum = jnp.stack(
        [jnp.sum(weights * grid_x[None, :], axis=1), jnp.sum(weights * grid_y[None, :], axis=1)],
        axis=0,
    )
    feat_sum = jnp.dot(weights.astype(jnp.bfloat16), keys, preferred_element_type=jnp.float32)
    return (top, total, coord_sum, feat_sum)


def per_device(source_feat, target_feat, proj):
    width = proj.shape[1]
    own_rows = source_feat.shape[0]
    tgt_rows = target_feat.shape[0]
    strips = lax.axis_size("tgt")
    queries = jnp.dot(source_feat, proj, preferred_element_type=jnp.float32).astype(jnp.bfloat16)
    keys = jnp.dot(
        lax.all_gather(target_feat, "src", axis=1, tiled=True),
        proj,
        preferred_element_type=jnp.float32,
    ).astype(jnp.bfloat16)
    own_start = (lax.axis_index("src") * strips + lax.axis_index("tgt")) * own_rows
    strip = lax.all_gather(queries, "tgt", axis=0, tiled=True)
    strip_rows = strip.shape[0]
    block = min(256, strip_rows)
    key_start = lax.axis_index("tgt") * tgt_rows

    def one_block(qblock):
        return partial_block(qblock, keys, key_start)

    top, total, coord_sum, feat_sum = lax.map(
        one_block, strip.reshape(strip_rows // block, block, width)
    )
    top = top.reshape(strip_rows)
    total = total.reshape(strip_rows)
    coord_sum = jnp.moveaxis(coord_sum, 1, 0).reshape(2, strip_rows)
    feat_sum = feat_sum.reshape(strip_rows, width)
    largest = lax.pmax(top, "tgt")
    rescale = jnp.exp(top - largest)
    total, coord_sum, feat_sum = (
        lax.psum_scatter(total * rescale, "tgt", scatter_dimension=0, tiled=True),
        lax.psum_scatter(coord_sum * rescale[None, :], "tgt", scatter_dimension=1, tiled=True),
        lax.psum_scatter(feat_sum * rescale[:, None], "tgt", scatter_dimension=0, tiled=True),
    )
    own_pos = own_start + jnp.arange(own_rows, dtype=jnp.int32)
    own_x, own_y = grid_coords(own_pos)
    flow = jnp.stack([coord_sum[0] / total - own_x, coord_sum[1] / total - own_y], axis=0)
    matched = (feat_sum / total[:, None]).astype(jnp.bfloat16)
    return (flow, matched)


def solution(mesh):
    in_specs = (P(("src", "tgt"), None), P("tgt", "src"), P())
    out_specs = (P(None, ("src", "tgt")), P(("src", "tgt"), None))
    return jax.shard_map(
        per_device, mesh=mesh, in_specs=in_specs, out_specs=out_specs, check_vma=False
    )
```

profile of v0, /device:TPU:0, one launch (start us, length us, event | category | flops | bytes accessed | tf_op | source)
XLA Modules:
  0.0 709.4 jit_solution(2130675689377072865)
XLA Ops:
  8.1 1.6 convolution_convert_fusion.1
  9.8 10.0 %all_gather.7 = bf16[1800,256]{0,1:T(8,128)(2,1)S(1)} all-gather(bf16[1800,64]{0,1:T(8,128)(2,1)} %param.6), channel_id=1, replica_groups=mesh['src'=4,'tgt'=32] {'src'}, dimensions={1}, use_global_device_ids=true | all-gather | bytes 1152000 | tf_op jit(solution)/shard_map/all_gather | solution.py:41
  20.2 64.7 %all-gather.2.cloned.1.call-done = bf16[4096,256]{1,0:T(8,128)(2,1)} async-done(((bf16[128,256]{1,0:T(8,128)(2,1)}), bf16[4096,256]{1,0:T(8,128)(2,1)}) %all-gather.2.cloned.1.call-update) | async-done | bytes 2097168 | tf_op jit(solution)/shard_map/all_gather | solution.py:46
  84.9 61.6 %while.18 = (s32[]{:T(128)}, f32[16,256]{1,0:T(8,128)S(1)}, f32[16,256]{1,0:T(8,128)S(1)}, f32[16,2,256]{2,1,0:T(2,128)S(1)}, f32[16,256,256]{2,1,0:T(8,128)}, /...) while((s32[]{:T(128)}, f32[16,256]{1,0:T(8,128)S(1)}, ...), condition=%wide.region_5.6_spmd, body=%wide.region_0.5_spmd.sunk | while | flops 476497280 | bytes 7810293 | solution.py:54
  88.7 1.4 fusion.44
  92.6 1.4 fusion.44
  96.4 1.4 fusion.44
  100.3 1.4 fusion.44
  104.1 1.4 fusion.44
  108.0 1.4 fusion.44
  111.9 1.4 fusion.44
  115.7 1.4 fusion.44
  119.6 1.4 fusion.44
  123.4 1.4 fusion.44
  127.3 1.4 fusion.44
  131.1 1.4 fusion.44
  138.8 1.4 fusion.44
  142.7 1.4 fusion.44
  146.5 180.2 %pmax.7 = f32[4096]{0:T(1024)S(1)} all-reduce(f32[4096]{0:T(1024)S(1)} %bitcast.74), channel_id=1, replica_groups=mesh['src'=4,'tgt'=32] {'tgt'}, use_global_device_ids=true, to_apply=%region_6.7 | all-reduce | flops 4096 | bytes 32768 | tf_op jit(solution)/shard_map/pmax | solution.py:61
  326.8 2.1 copy.5
  329.0 3.9 bitcast_multiply_fusion
  334.8 176.2 %all-reduce = f32[4096]{0:T(1024)S(1)} all-reduce(f32[4096]{0:T(1024)S(1)} %get-tuple-element.134), channel_id=3, replica_groups=mesh['src'=4,'tgt'=32] {'tgt'}, use_global_device_ids=true, to_apply=%region_8.9.clone | all-reduce | flops 4096 | bytes 32768
  513.2 188.0 %reduce-scatter.5.cloned.1.call-done = f32[128,256]{1,0:T(8,128)} async-done(((f32[4096,256]{1,0:T(8,128)}), f32[128,256]{1,0:T(8,128)}) %reduce-scatter.5.cloned.1.call-update) | async-done | bytes 131088 | tf_op jit(solution)/shard_map/reduce_scatter | solution.py:66
  701.2 1.6 divide_convert_fusion
  (125 shorter events, 46.2 us)
Async XLA Ops:
  7.2 0.9 copy-start
  7.2 77.7 %all-gather.2.cloned.1.call-start = ((), (), s32[]{:S(2)}) async-start(), calls=%async_computation.2 | async-start | bytes 2162688 | tf_op jit(solution)/shard_map/all_gather | solution.py:46
  9.7 501.6 %reduce-scatter.7.cloned.1.call-start = ((), (), s32[]{:S(2)}) async-start(), calls=%async_computation.4 | async-start | bytes 2162688
  328.9 372.3 %reduce-scatter.5.cloned.1.call-start = ((), (), s32[]{:S(2)}) async-start(), calls=%async_computation.3 | async-start | bytes 4325376 | tf_op jit(solution)/shard_map/reduce_scatter | solution.py:66
  332.9 0.7 copy-start.1
Sparse Core Ops, SparseCore 0:
  11.7 73.2 all-gather.1
  329.0 182.2 reduce-scatter.6
  513.9 187.2 reduce-scatter.4
where the time goes:
time: 710 us; the launch traced here: 709 us
  blocking collectives  366 us (52%)
  waiting for transfers between devices  253 us (36%)
  matrix products  44.9 us (6%)
  other arithmetic  23.4 us (3%)
  between operations  14.5 us (2%)
    reduce_scatter x1, waiting for transfers between devices, per_device(): lax.psum_scatter(feat_sum * rescale[:, None], 'tgt', scatter_dimension=0,...  188 us
    pmax x1, blocking collectives, per_device(): largest = lax.pmax(top, 'tgt')  180 us
    unnamed x1, blocking collectives  176 us
    all_gather x1, waiting for transfers between devices, per_device(): strip = lax.all_gather(queries, 'tgt', axis=0, tiled=True)  64.7 us
    dot_general x16, matrix products, partial_block(): jnp.einsum('qc,kc->qk', queries, keys, preferred_element_type=jnp.float32)  22.6 us
    dot_general x16, matrix products, partial_block(): jnp.dot(weights.astype(jnp.bfloat16), keys, preferred_element_type=jnp.fl...  20.2 us
    reduce_sum x16, other arithmetic, partial_block(): jnp.sum(weights * grid_x[None, :], axis=1)  16.6 us
  transfers between devices with their start and end apart: 3, of which 3 were waited for; matrix products, arithmetic and copies ran while one was open for 1% of the time, Pallas kernels for 0%

commit v1 on v0

--- a/solution.py
+++ b/solution.py
@@ -43,7 +43,16 @@
         preferred_element_type=jnp.float32,
     ).astype(jnp.bfloat16)
     own_start = (lax.axis_index("src") * strips + lax.axis_index("tgt")) * own_rows
-    strip = lax.all_gather(queries, "tgt", axis=0, tiled=True)
+
+    def lay_the_desk(t0):
+        pieces_in = []
+        for _ in range(jax.lax.axis_size("tgt")):
+            pieces_in.append(t0)
+        everything = jnp.stack(pieces_in)
+        arr_now = jax.lax.all_to_all(everything, axis_name="tgt", split_axis=0, concat_axis=0)
+        return jnp.concatenate(arr_now, 0)
+
+    strip = lay_the_desk(queries)
     strip_rows = strip.shape[0]
     block = min(256, strip_rows)
     key_start = lax.axis_index("tgt") * tgt_rows

time: 710 us -> 679 us (0.956)
  waiting for transfers between devices: 253 us -> 187 us
  blocking collectives: 366 us -> 389 us
  starting transfers between devices: 0.12 us -> 11.2 us
    all_gather x1 -> x0, waiting for transfers between devices: 64.7 us -> none  [per_device(): strip = lax.all_gather(queries, 'tgt', axis=0, tiled=True)]
    all_gather x1, blocking collectives: 9.96 us -> 29.4 us  [per_device(): lax.all_gather(target_feat, 'src', axis=1, tiled=True)]
    all_to_all x0 -> x1, starting transfers between devices: none -> 11.1 us  [lay_the_desk(): jax.lax.all_to_all(everything, axis_name='tgt', split_axis=0, concat_axis=0)]
  transfers between devices with their start and end apart: 3 -> 3, of which waited for: 3 -> 2; matrix products, arithmetic and copies ran while one was open for 1% -> 1% of each run, Pallas kernels for 0% -> 0%
where the time goes in v1:
time: 679 us
  blocking collectives  389 us (57%)
  waiting for transfers between devices  187 us (28%)
  matrix products  44.3 us (7%)
  other arithmetic  23.4 us (3%)
  between operations  14.8 us (2%)
  starting transfers between devices  11.2 us (2%)
  local copies, waits for them, and re-layouts  7.93 us (1%)
    reduce_scatter x1, waiting for transfers between devices, per_device(): lax.psum_scatter(feat_sum * rescale[:, None], 'tgt', scatter_dimension=0,...  187 us
    pmax x1, blocking collectives, per_device(): largest = lax.pmax(top, 'tgt')  184 us
    unnamed x1, blocking collectives  176 us
    all_gather x1, blocking collectives, per_device(): lax.all_gather(target_feat, 'src', axis=1, tiled=True)  29.4 us
    dot_general x16, matrix products, partial_block(): jnp.einsum('qc,kc->qk', queries, keys, preferred_element_type=jnp.float32)  22.7 us
    dot_general x16, matrix products, partial_block(): jnp.dot(weights.astype(jnp.bfloat16), keys, preferred_element_type=jnp.fl...  20.2 us
    reduce_sum x16, other arithmetic, partial_block(): jnp.sum(weights * grid_x[None, :], axis=1)  16.6 us
  transfers between devices with their start and end apart: 3, of which 2 were waited for; matrix products, arithmetic and copies ran while one was open for 1% of the time, Pallas kernels for 0%

profile of v1, /device:TPU:0, one launch (start us, length us, event | category | flops | bytes accessed | tf_op | source)
XLA Modules:
  0.0 678.6 jit_solution(1946889032732983868)
XLA Ops:
  9.1 1.5 stack.23
  10.6 11.1 %all-to-all-start = ((bf16[32,128,256]{2,1,0:T(8,128)(2,1)}), bf16[32,128,256]{2,1,0:T(8,128)(2,1)}, u32[]{:S(2)}, u32[]{:S(2)}) async-start(bf16[32,128,256]{2,1,0:T(8,128)(2,1)} %stack.23), calls=%async_computation | async-start | bytes 4194304 | tf_op jit(solution)/shard_map/all_to_all | solution.py:52
  21.9 29.4 %all_gather.3 = bf16[1800,256]{0,1:T(8,128)(2,1)S(1)} all-gather(bf16[1800,64]{0,1:T(8,128)(2,1)S(1)} %copy-done.1), channel_id=1, replica_groups=mesh['src'=4,'tgt'=32] {'src'}, dimensions={1}, use_global_device_ids=true | all-gather | bytes 1152000 | tf_op jit(solution)/shard_map/all_gather | solution.py:41
  52.3 61.7 %while.18 = (s32[]{:T(128)}, f32[16,256]{1,0:T(8,128)S(1)}, f32[16,256]{1,0:T(8,128)S(1)}, f32[16,2,256]{2,1,0:T(2,128)S(1)}, f32[16,256,256]{2,1,0:T(8,128)}, /...) while((s32[]{:T(128)}, f32[16,256]{1,0:T(8,128)S(1)}, ...), condition=%wide.region_5.6_spmd, body=%wide.region_0.5_spmd.sunk | while | flops 476497280 | bytes 7810293 | solution.py:63
  52.3 1.4 fusion.44
  56.1 1.4 fusion.44
  60.0 1.4 fusion.44
  63.8 1.4 fusion.44
  67.7 1.4 fusion.44
  75.4 1.4 fusion.44
  79.3 1.4 fusion.44
  87.0 1.4 fusion.44
  90.8 1.4 fusion.44
  94.7 1.4 fusion.44
  98.6 1.4 fusion.44
  102.4 1.4 fusion.44
  106.3 1.4 fusion.44
  110.1 1.4 fusion.44
  114.0 183.6 %pmax.7 = f32[4096]{0:T(1024)S(1)} all-reduce(f32[4096]{0:T(1024)S(1)} %bitcast.73), channel_id=1, replica_groups=mesh['src'=4,'tgt'=32] {'tgt'}, use_global_device_ids=true, to_apply=%region_6.7 | all-reduce | flops 4096 | bytes 32768 | tf_op jit(solution)/shard_map/pmax | solution.py:70
  297.7 2.1 copy.5
  299.8 3.9 bitcast_multiply_fusion
  305.6 176.2 %all-reduce = f32[4096]{0:T(1024)S(1)} all-reduce(f32[4096]{0:T(1024)S(1)} %get-tuple-element.134), channel_id=3, replica_groups=mesh['src'=4,'tgt'=32] {'tgt'}, use_global_device_ids=true, to_apply=%region_8.9.clone | all-reduce | flops 4096 | bytes 32768
  483.6 186.6 %reduce-scatter.5.cloned.1.call-done = f32[128,256]{1,0:T(8,128)} async-done(((f32[4096,256]{1,0:T(8,128)}), f32[128,256]{1,0:T(8,128)}) %reduce-scatter.5.cloned.1.call-update) | async-done | bytes 131088 | tf_op jit(solution)/shard_map/reduce_scatter | solution.py:75
  670.2 1.6 divide_convert_fusion
  (127 shorter events, 47.5 us)
Async XLA Ops:
  7.2 0.9 copy-start
  10.6 11.2 %copy-start.1 = (bf16[1800,64]{0,1:T(8,128)(2,1)S(1)}, bf16[1800,64]{0,1:T(8,128)(2,1)}, u32[]{:S(2)}) copy-start(bf16[1800,64]{0,1:T(8,128)(2,1)} %param.6) | copy-start | bytes 691204
  10.6 41.7 %all-to-all-start = ((bf16[32,128,256]{2,1,0:T(8,128)(2,1)}), bf16[32,128,256]{2,1,0:T(8,128)(2,1)}, u32[]{:S(2)}, u32[]{:S(2)}) async-start(bf16[32,128,256]{2,1,0:T(8,128)(2,1)} %stack.23), calls=%async_computation | async-start | bytes 4194304 | tf_op jit(solution)/shard_map/all_to_all | solution.py:52
  21.8 460.0 %reduce-scatter.7.cloned.1.call-start = ((), (), s32[]{:S(2)}) async-start(), calls=%async_computation.4 | async-start | bytes 2162688
  299.8 370.4 %reduce-scatter.5.cloned.1.call-start = ((), (), s32[]{:S(2)}) async-start(), calls=%async_computation.3 | async-start | bytes 4325376 | tf_op jit(solution)/shard_map/reduce_scatter | solution.py:75
  303.7 0.7 copy-start.2
Sparse Core Ops, SparseCore 0:
  299.9 180.7 reduce-scatter.6
  483.2 186.9 reduce-scatter.4
